TPU v7x, 128 devices: a whole 4x4x4 slice. The times are simulated.
128 devices in a mesh: tok: 8 (over x, core), head: 8 (over y, z_hi), seq: 2 (over z_lo).
Axes of the slice: x: 4, y: 4, z: 4 (z_hi: 2, z_lo: 2; z = z_hi * 2 + z_lo), core: 2. Of those that a mesh axis runs over, the one named last changes fastest.
Arguments:
- queries: bfloat16 [2, 8192, 4096], P('seq', ('tok', 'head')), may hold values from -6 to 6
- keys: bfloat16 [2, 8192, 4096], P('seq', ('tok', 'head')), may hold values from -6 to 6
- values: bfloat16 [2, 8192, 4096], P('seq', ('tok', 'head')), may hold values from -6 to 6
- rates: float32 [2, 8, 8192], P('seq', 'head', 'tok'), may hold values from 0.00011048543 to 0.0011048544
- fast_one: float32 [8, 512, 512], P('head'), may hold values from -0.25 to 0.25
- fast_two: float32 [8, 512, 512], P('head'), may hold values from -0.25 to 0.25
- fast_three: float32 [8, 512, 512], P('head'), may hold values from -0.25 to 0.25
- grad_out: bfloat16 [2, 8192, 4096], P('seq', ('tok', 'head')), may hold values from -6 to 6
Outputs:
- grad_queries: bfloat16 [2, 8192, 4096], P('seq', ('tok', 'head'))
- grad_keys: bfloat16 [2, 8192, 4096], P('seq', ('tok', 'head'))
- grad_values: bfloat16 [2, 8192, 4096], P('seq', ('tok', 'head'))
- grad_rates: float32 [2, 8, 8192], P('seq', 'head', 'tok')
- grad_fast_one: float32 [8, 512, 512], P('head')
- grad_fast_two: float32 [8, 512, 512], P('head')
- grad_fast_three: float32 [8, 512, 512], P('head')
All inputs are finite; a program needn't handle non-finite values.
Results may differ from a plain program's by a relative error of at most 0.016.
Values may be sent and summed in bfloat16 or wider, within the bound.
A program may use at most 128 MiB of HBM per device.

v0:
```python
import jax
import jax.numpy as jnp
from jax import lax
from jax.sharding import PartitionSpec as P

epsilon = 1e-06


def side_by_side(arrays, axis, split_dim, concat_dim, along):
    ends, at = ([], 0)
    for a in arrays[:-1]:
        at += a.shape[along]
        ends.append(at)
    both = jnp.concatenate(arrays, axis=along)
    return tuple(
        jnp.split(
            lax.all_to_all(both, axis, split_axis=split_dim, concat_axis=concat_dim, tiled=True),
            ends,
            axis=along,
        )
    )


def shortened(value):

    def short(part):
        return part.astype(jnp.bfloat16) if part.dtype == jnp.float32 else part

    return jax.tree.map(short, value)


def matmul(left, right):
    return jnp.dot(
        left.astype(jnp.bfloat16), right.astype(jnp.bfloat16), preferred_element_type=jnp.float32
    )


def matmul_tn(left, right):
    return lax.dot_general(
        left.astype(jnp.bfloat16),
        right.astype(jnp.bfloat16),
        (((0,), (0,)), ((), ())),
        preferred_element_type=jnp.float32,
    )


def matmul_nt(left, right):
    return lax.dot_general(
        left.astype(jnp.bfloat16),
        right.astype(jnp.bfloat16),
        (((1,), (1,)), ((), ())),
        preferred_element_type=jnp.float32,
    )


def activation(preact):
    squash = jax.nn.sigmoid(preact)
    swished = preact * squash
    slope_one = squash * (1.0 + preact * (1.0 - squash))
    slope_two = squash * (1.0 - squash) * (2.0 + preact * (1.0 - 2.0 * squash))
    return (squash, swished, slope_one, slope_two)


def inner_forward(keys_h, values_h, rate_h, w_one, w_two, w_three):
    pre_one = matmul(keys_h, w_one)
    pre_three = matmul(keys_h, w_three)
    parts = activation(pre_one)
    swished, slope_one = (parts[1], parts[2])
    hidden = swished * pre_three
    target = -rate_h[:, None] * values_h.astype(jnp.float32)
    grad_two = matmul_tn(hidden, target)
    back_hidden = matmul_nt(target, w_two)
    delta_one = back_hidden * pre_three * slope_one
    delta_three = back_hidden * swished
    grad_one = matmul_tn(keys_h, delta_one)
    grad_three = matmul_tn(keys_h, delta_three)
    saved = (pre_one, pre_three, target, back_hidden, delta_one, delta_three)
    return ((grad_one, grad_two, grad_three), saved)


def normalize(weight, update):
    ref_norm = jnp.sqrt(jnp.sum(weight * weight, axis=-2, keepdims=True) + epsilon)
    upd_norm = jnp.sqrt(jnp.sum(update * update, axis=-2, keepdims=True) + epsilon)
    return (update * (ref_norm / upd_norm), ref_norm, upd_norm)


def apply_backward(queries_h, cotangent, new_one, new_two, new_three):
    pre_one = matmul(queries_h, new_one)
    pre_three = matmul(queries_h, new_three)
    parts = activation(pre_one)
    swished, slope_one = (parts[1], parts[2])
    hidden = swished * pre_three
    grad_two = matmul_tn(hidden, cotangent)
    back_hidden = matmul_nt(cotangent, new_two)
    delta_one = back_hidden * pre_three * slope_one
    delta_three = back_hidden * swished
    grad_one = matmul_tn(queries_h, delta_one)
    grad_three = matmul_tn(queries_h, delta_three)
    grad_queries = matmul_nt(delta_one, new_one) + matmul_nt(delta_three, new_three)
    return ((grad_one, grad_two, grad_three), grad_queries)


def adjoint(weight, update, ref_norm, upd_norm, grad_new):
    moment = jnp.sum(grad_new * update, axis=-2, keepdims=True)
    factor = ref_norm / upd_norm
    grad_update = factor * grad_new - update * (factor * moment / (upd_norm * upd_norm))
    direct = weight * (moment / (upd_norm * ref_norm)) + grad_update
    return (-grad_update, direct)


def double_backward(
    keys_h, values_h, rate_h, w_one, w_two, w_three, saved, cot_one, cot_two, cot_three
):
    pre_one, pre_three, target, back_hidden, delta_one, delta_three = saved
    parts = activation(pre_one)
    swished, slope_one, slope_two = (parts[1], parts[2], parts[3])
    hidden = swished * pre_three
    grad_hidden = matmul_nt(target, cot_two)
    grad_target = matmul(hidden, cot_two)
    grad_delta_one = matmul(keys_h, cot_one)
    grad_delta_three = matmul(keys_h, cot_three)
    grad_keys = matmul_nt(delta_one, cot_one) + matmul_nt(delta_three, cot_three)
    grad_back = grad_delta_one * pre_three * slope_one + grad_delta_three * swished
    grad_pre_three = grad_delta_one * back_hidden * slope_one + grad_hidden * swished
    grad_pre_one = (
        grad_delta_one * back_hidden * pre_three * slope_two
        + grad_delta_three * back_hidden * slope_one
        + grad_hidden * pre_three * slope_one
    )
    grad_target = grad_target + matmul(grad_back, w_two)
    weight_two = matmul_tn(grad_back, target)
    grad_keys = grad_keys + (matmul_nt(grad_pre_one, w_one) + matmul_nt(grad_pre_three, w_three))
    weight_one = matmul_tn(keys_h, grad_pre_one)
    weight_three = matmul_tn(keys_h, grad_pre_three)
    grad_values = -rate_h[:, None] * grad_target
    grad_rate = -jnp.sum(values_h.astype(jnp.float32) * grad_target, axis=1)
    return (grad_keys, grad_values, grad_rate, (weight_one, weight_two, weight_three))


def body(queries, keys, values, rates, fast_one, fast_two, fast_three, grad_out):
    heads = fast_one.shape[0]
    width = fast_one.shape[1]
    weights = (fast_one, fast_two, fast_three)
    key_local, value_local = side_by_side((keys, values), "head", 2, 1, 0)
    inner_list, saved_list = ([], [])
    head_idx = 0
    start = head_idx * width
    inner, saved = inner_forward(
        key_local[0, :, start : start + width],
        value_local[0, :, start : start + width],
        rates[0, head_idx],
        fast_one[head_idx],
        fast_two[head_idx],
        fast_three[head_idx],
    )
    inner_list.append(inner)
    saved_list.append(saved)
    partial_inner = tuple((jnp.stack([inner_list[0][index]]) for index in range(3)))
    summed_inner = lax.psum(partial_inner, "tok")
    query_local, cot_local = side_by_side((queries, grad_out), "head", 2, 1, 0)
    updates = [weights[index] - summed_inner[index] for index in range(3)]
    normed = [normalize(weights[index], updates[index]) for index in range(3)]
    new_list, query_heads = ([], [])
    head_idx = 0
    start = head_idx * width
    grads_new, grad_queries = apply_backward(
        query_local[0, :, start : start + width],
        cot_local[0, :, start : start + width],
        normed[0][0][head_idx],
        normed[1][0][head_idx],
        normed[2][0][head_idx],
    )
    new_list.append(grads_new)
    query_heads.append(grad_queries)
    partial_new = tuple((jnp.stack([new_list[0][index]]) for index in range(3)))
    query_block = query_heads[0].astype(jnp.bfloat16)[None]
    query_back = lax.all_to_all(query_block, "head", split_axis=1, concat_axis=2, tiled=True)
    summed_new = lax.psum(partial_new, "tok")
    keep_flag = (lax.axis_index("tok") == 0).astype(jnp.float32)
    results = [
        adjoint(
            weights[index], updates[index], normed[index][1], normed[index][2], summed_new[index]
        )
        for index in range(3)
    ]
    cotangents = [results[index][0] for index in range(3)]
    directs = [results[index][1] * keep_flag for index in range(3)]
    key_heads, value_heads, rate_heads, extra_list = ([], [], [], [])
    head_idx = 0
    start = head_idx * width
    grad_keys, grad_values, grad_rate, extra = double_backward(
        key_local[0, :, start : start + width],
        value_local[0, :, start : start + width],
        rates[0, head_idx],
        fast_one[head_idx],
        fast_two[head_idx],
        fast_three[head_idx],
        saved_list[head_idx],
        cotangents[0][head_idx],
        cotangents[1][head_idx],
        cotangents[2][head_idx],
    )
    key_heads.append(grad_keys.astype(jnp.bfloat16))
    value_heads.append(grad_values.astype(jnp.bfloat16))
    rate_heads.append(grad_rate)
    extra_list.append(extra)
    partial_weights = tuple(
        (directs[index] + jnp.stack([extra_list[0][index]]) for index in range(3))
    )
    total_one, total_two, total_three = jax.tree.map(
        lambda part: part.astype(jnp.float32), lax.psum(shortened(partial_weights), ("tok", "seq"))
    )
    key_block = key_heads[0][None]
    value_block = value_heads[0][None]
    key_back, value_back = side_by_side((key_block, value_block), "head", 1, 2, 0)
    rate_grads = jnp.stack(rate_heads)[None]
    return (query_back, key_back, value_back, rate_grads, total_one, total_two, total_three)


def solution(mesh):
    placed = (
        P("seq", ("tok", "head"), None),
        P("seq", ("tok", "head"), None),
        P("seq", ("tok", "head"), None),
        P("seq", "head", "tok"),
        P("head", None, None),
        P("head", None, None),
        P("head", None, None),
        P("seq", ("tok", "head"), None),
    )
    return jax.shard_map(
        body,
        mesh=mesh,
        in_specs=placed,
        out_specs=(
            P("seq", ("tok", "head"), None),
            P("seq", ("tok", "head"), None),
            P("seq", ("tok", "head"), None),
            P("seq", "head", "tok"),
            P("head", None, None),
            P("head", None, None),
            P("head", None, None),
        ),
        check_vma=False,
    )
```

profile of v0, /device:TPU:1, one launch (start us, length us, event | category | flops | bytes accessed | tf_op | source)
XLA Modules:
  0.0 484.6 jit_solution(5529471393245594606)
XLA Ops:
  7.2 1.7 pad_maximum_fusion.1
  8.9 3.8 copy.86
  12.7 8.5 %all-to-all-start.1 = ((bf16[2,128,4096]{1,0,2:T(2,128)(2,1)}), bf16[2,128,4096]{1,0,2:T(2,128)(2,1)}, u32[]{:S(2)}, u32[]{:S(2)}) async-start(bf16[2,128,4096]{1,0,2:T(2,128)(2,1)} %copy.86), calls=%async_computation.1 | async-start | bytes 4194304 | tf_op jit(solution)/shard_map/all_to_all | solution.py:17
  21.2 2.8 copy.82
  24.0 5.5 %copy.83 = bf16[1,128,4096]{1,0,2:T(2,128)(2,1)} copy(bf16[1,128,4096]{2,1,0:T(8,128)(2,1)} %param.15) | data formatting | bytes 2097152 | tf_op args[7]
  29.5 6.4 %pad_maximum_fusion = bf16[2,128,4096]{1,0,2:T(2,128)(2,1)} fusion(bf16[1,128,4096]{1,0,2:T(2,128)(2,1)} %copy.83, bf16[1,128,4096]{1,0,2:T(2,128)(2,1)S(1)} %copy.82), kind=kLoop, calls=%fused_computation.9 | loop fusion | flops 4194304 | bytes 4194304 | tf_op jit(solution)/shard_map/concatenate | solution.py:14
  35.9 15.9 %all-to-all-done.1 = bf16[2,128,4096]{1,0,2:T(2,128)(2,1)} async-done(((bf16[2,128,4096]{1,0,2:T(2,128)(2,1)}), bf16[2,128,4096]{1,0,2:T(2,128)(2,1)}, u32[]{:S(2)}, u32[]{:S(2)}) %all-to-all-start.1) | async-done | bytes 2097184 | tf_op jit(solution)/shard_map/all_to_all | solution.py:17
  51.9 4.4 all-to-all-start
  56.3 4.7 copy.87
  61.1 1.9 copy-done.2
  65.6 1.4 copy-done.13
  67.0 3.1 multiply_convert_fusion.5
  70.1 1.7 convolution_bitcast_fusion.6
  73.1 1.7 convolution_bitcast_fusion.8
  74.9 11.1 %all-to-all-done = bf16[2,128,4096]{1,0,2:T(2,128)(2,1)} async-done(((bf16[2,128,4096]{1,0,2:T(2,128)(2,1)}), bf16[2,128,4096]{1,0,2:T(2,128)(2,1)}, u32[]{:S(2)}, u32[]{:S(2)}) %all-to-all-start) | async-done | bytes 2097184 | tf_op jit(solution)/shard_map/all_to_all | solution.py:17
  86.0 1.9 copy.84
  90.7 3.0 convolution_bitcast_fusion.7
  93.7 47.7 %all-reduce.13.cloned.1.call-done = (f32[1,512,512]{2,1,0:T(8,128)}, f32[1,512,512]{2,1,0:T(8,128)}) async-done(((f32[1,512,512]{2,1,0:T(8,128)}, f32[1,512,512]{2,1,0:T(8,128)}), (f32[1,512,512]{2,1,0:T(8,128)}, f32[1,512,512]{2,1,0:T(8,128)})) %all-reduce.13.cloned.1.call-update) | async-done | bytes 2097168 | tf_op jit(solution)/shard_map/psum | solution.py:159
  141.4 2.5 multiply_reduce_fusion.3
  145.5 2.3 multiply_convert_fusion.2
  148.7 1.7 convolution_bitcast_fusion.4
  150.7 65.3 %all-reduce.11.cloned.1.call-done = (f32[1,512,512]{2,1,0:T(8,128)}, f32[1,512,512]{2,1,0:T(8,128)}) async-done(((f32[1,512,512]{2,1,0:T(8,128)}, f32[1,512,512]{2,1,0:T(8,128)}), (f32[1,512,512]{2,1,0:T(8,128)}, f32[1,512,512]{2,1,0:T(8,128)})) %all-reduce.11.cloned.1.call-update) | async-done | bytes 2097168 | tf_op jit(solution)/shard_map/psum | solution.py:159
  216.0 2.4 multiply_reduce_fusion.1
  218.8 2.8 multiply_convert_fusion.3
  221.6 1.7 convolution_bitcast_fusion.5
  223.4 2.1 fusion.47
  225.5 1.8 convolution_bitcast_fusion.3
  227.3 2.7 fusion.12
  230.0 3.0 copy.101
  233.5 9.0 %reduce.9 = bf16[1024,512]{1,0:T(8,128)(2,1)} reduce(bf16[1024,1,512]{2,1,0:T(2,128)(2,1)} %bitcast.164, bf16[]{:T(256)} %broadcast.129), dimensions={1}, to_apply=%bitcast.149.reduce_sub_computation | reduce | bytes 2097154
  242.5 2.8 reshape.255
  245.3 6.6 %all-to-all-start.2 = ((bf16[8,2,32768]{2,1,0:T(2,128)(2,1)}), bf16[8,2,32768]{2,1,0:T(2,128)(2,1)}, u32[]{:S(2)}, u32[]{:S(2)}) async-start(bf16[8,2,32768]{2,1,0:T(2,128)(2,1)} %reshape.255), calls=%async_computation.2 | async-start | bytes 2097152 | tf_op jit(solution)/shard_map/all_to_all | solution.py:177
  251.9 1.5 fusion.27
  253.4 2.1 fusion.62
  255.5 2.1 fusion.60
  257.6 35.5 %all-reduce.9.cloned.1.call-done = (f32[1,512,512]{2,1,0:T(8,128)}, f32[1,512,512]{2,1,0:T(8,128)}) async-done(((f32[1,512,512]{2,1,0:T(8,128)}, f32[1,512,512]{2,1,0:T(8,128)}), (f32[1,512,512]{2,1,0:T(8,128)}, f32[1,512,512]{2,1,0:T(8,128)})) %all-reduce.9.cloned.1.call-update) | async-done | bytes 2097168 | tf_op jit(solution)/shard_map/psum | solution.py:178
  293.1 1.5 multiply_reduce_fusion.2
  301.4 2.7 add_convert_fusion.2
  309.5 3.5 copy.93
  313.0 1.6 fusion.17
  314.6 1.6 fusion.18
  316.2 6.7 %all-to-all-start.3 = ((bf16[2,1024,512]{2,0,1:T(2,128)(2,1)}), bf16[2,1024,512]{2,0,1:T(2,128)(2,1)}, u32[]{:S(2)}, u32[]{:S(2)}) async-start(bf16[2,1024,512]{2,0,1:T(2,128)(2,1)} %copy.93), calls=%async_computation.3 | async-start | bytes 4194304 | tf_op jit(solution)/shard_map/all_to_all | solution.py:17
  323.0 3.1 fusion.19
  326.2 4.6 reshape.256
  333.6 128.1 %all-reduce.15.cloned.1.call-done = (bf16[1,512,512]{2,1,0:T(8,128)(2,1)}, bf16[1,512,512]{2,1,0:T(8,128)(2,1)}, bf16[1,512,512]{2,1,0:T(8,128)(2,1)}) async-done(((bf16[1,512,512]{2,1,0:T(8,128)(2,1)}, bf16[1,512,512]{2,1,0:T(8,128)(2,1)}, bf16[1,512,512]{2,1,0:T(8,128)(2,1)}), (bf16[1,512,512]{2,1,0:T(8,128)(2,1)}, bf16[1,512,512]{2,1,0:T(8,128)(2,1)}, ...) | async-done | bytes 1572880 | tf_op jit(solution)/shard_map/psum | solution.py:211
  461.7 2.2 convert_element_type.196
  463.9 2.1 convert_element_type.198
  467.2 5.5 %fusion.55 = (bf16[1,128,8,512]{3,0,1,2:T(2,128)(2,1)S(1)}, bf16[1,128,8,512]{3,0,1,2:T(2,128)(2,1)S(1)}) fusion(bf16[2,128,8,512]{3,0,1,2:T(2,128)(2,1)} %bitcast.33), kind=kLoop, calls=%fused_computation.110 | loop fusion | bytes 4194304 | tf_op jit(solution)/shard_map/split | solution.py:16
  (127 shorter events, 31.4 us)
Async XLA Ops:
  12.7 8.5 %copy-start.40 = (f32[1,1,1024]{2,1,0:T(1,128)S(1)}, f32[1,1,1024]{2,1,0:T(1,128)}, u32[]{:S(2)}) copy-start(f32[1,1,1024]{2,1,0:T(1,128)} %param.11) | copy-start | bytes 12292
  12.7 8.5 %copy-start.28 = (bf16[1,128,4096]{2,1,0:T(8,128)(2,1)S(1)}, bf16[1,128,4096]{2,1,0:T(8,128)(2,1)}, u32[]{:S(2)}) copy-start(bf16[1,128,4096]{2,1,0:T(8,128)(2,1)} %param.8) | copy-start | bytes 3145732
  12.7 39.2 %all-to-all-start.1 = ((bf16[2,128,4096]{1,0,2:T(2,128)(2,1)}), bf16[2,128,4096]{1,0,2:T(2,128)(2,1)}, u32[]{:S(2)}, u32[]{:S(2)}) async-start(bf16[2,128,4096]{1,0,2:T(2,128)(2,1)} %copy.86), calls=%async_computation.1 | async-start | bytes 4194304 | tf_op jit(solution)/shard_map/all_to_all | solution.py:17
  51.9 34.2 %all-to-all-start = ((bf16[2,128,4096]{1,0,2:T(2,128)(2,1)}), bf16[2,128,4096]{1,0,2:T(2,128)(2,1)}, u32[]{:S(2)}, u32[]{:S(2)}) async-start(bf16[2,128,4096]{1,0,2:T(2,128)(2,1)} %pad_maximum_fusion), calls=%async_computation | async-start | bytes 4194304 | tf_op jit(solution)/shard_map/all_to_all | solution.py:17
  56.2 85.1 %all-reduce.13.cloned.1.call-start = ((), (), s32[]{:S(2)}) async-start(), calls=%async_computation.6 | async-start | bytes 4194304 | tf_op jit(solution)/shard_map/psum | solution.py:159
  61.0 10.8 %copy-start = (bf16[2,128,8,512]{3,1,2,0:T(8,128)(2,1)}, bf16[2,128,8,512]{3,1,2,0:T(8,128)(2,1)S(1)}, u32[]{:S(2)}) copy-start(bf16[2,128,8,512]{3,1,2,0:T(8,128)(2,1)S(1)} %copy.87) | copy-start | bytes 6291460
  61.0 2.0 copy-start.2
  63.0 1.2 copy-start.6
  64.2 1.4 copy-start.22
  64.9 5.2 %copy-start.24 = (f32[1024,512]{1,0:T(8,128)}, f32[1024,512]{1,0:T(8,128)S(1)}, u32[]{:S(2)}) copy-start(f32[1024,512]{1,0:T(8,128)S(1)} %fusion.37) | copy-start | bytes 6291460
  64.9 2.0 copy-start.13
  65.3 4.8 copy-start.35
  70.1 1.7 copy-start.31
  70.1 2.0 copy-start.29
  72.1 1.0 copy-start.16
  74.8 141.2 %all-reduce.11.cloned.1.call-start = ((), (), s32[]{:S(2)}) async-start(), calls=%async_computation.5 | async-start | bytes 4194304 | tf_op jit(solution)/shard_map/psum | solution.py:159
  90.7 50.7 %copy-start.7 = (f32[1,512,512]{2,1,0:T(8,128)S(1)}, f32[1,512,512]{2,1,0:T(8,128)}, u32[]{:S(2)}) copy-start(f32[1,512,512]{2,1,0:T(8,128)} %param.12) | copy-start | bytes 3145732
  141.4 2.5 copy-start.19
  143.8 1.0 copy-start.4
  143.9 1.6 copy-start.37
  144.6 3.1 copy-start.26
  150.5 142.6 %all-reduce.9.cloned.1.call-start = ((), (), s32[]{:S(2)}) async-start(), calls=%async_computation.4 | async-start | bytes 4194304 | tf_op jit(solution)/shard_map/psum | solution.py:178
  216.0 2.4 copy-start.20
  216.0 2.9 copy-start.27
  223.3 2.1 copy-start.38
  245.3 70.9 %all-to-all-start.2 = ((bf16[8,2,32768]{2,1,0:T(2,128)(2,1)}), bf16[8,2,32768]{2,1,0:T(2,128)(2,1)}, u32[]{:S(2)}, u32[]{:S(2)}) async-start(bf16[8,2,32768]{2,1,0:T(2,128)(2,1)} %reshape.255), calls=%async_computation.2 | async-start | bytes 2097152 | tf_op jit(solution)/shard_map/all_to_all | solution.py:177
  253.4 2.1 copy-start.33
  293.1 1.5 copy-start.11
  294.9 1.2 copy-start.32
  294.9 4.7 copy-start.41
  296.1 1.2 copy-start.5
  296.1 1.5 copy-start.12
  297.7 1.2 copy-start.30
  297.7 1.9 copy-start.36
  298.0 1.9 copy-start.23
  298.0 2.5 copy-start.25
  298.9 2.5 copy-start.21
  301.4 2.7 copy-start.8
  304.1 2.0 copy-start.1
  304.1 2.2 copy-start.14
  306.4 1.2 copy-start.3
  306.4 1.9 copy-start.15
  309.4 3.5 copy-start.10
  313.0 1.7 copy-start.17
  316.2 6.8 %copy-start.9 = (f32[1,512,512]{2,1,0:T(8,128)S(1)}, f32[1,512,512]{2,1,0:T(8,128)}, u32[]{:S(2)}) copy-start(f32[1,512,512]{2,1,0:T(8,128)} %param.12) | copy-start | bytes 3145732
  316.2 150.9 %all-to-all-start.3 = ((bf16[2,1024,512]{2,0,1:T(2,128)(2,1)}), bf16[2,1024,512]{2,0,1:T(2,128)(2,1)}, u32[]{:S(2)}, u32[]{:S(2)}) async-start(bf16[2,1024,512]{2,0,1:T(2,128)(2,1)} %copy.93), calls=%async_computation.3 | async-start | bytes 4194304 | tf_op jit(solution)/shard_map/all_to_all | solution.py:17
  323.0 138.7 %all-reduce.15.cloned.1.call-start = ((), (), s32[]{:S(2)}) async-start(), calls=%async_computation.7 | async-start | bytes 3145728 | tf_op jit(solution)/shard_map/psum | solution.py:211
  461.7 4.4 copy-start.39
  (2 other events, 1.9 us)
Sparse Core Ops, SparseCore 0:
  74.9 66.3 all-reduce.12
  150.6 65.3 all-reduce.10
  227.4 65.6 all-reduce.8
  326.8 134.8 all-reduce.14
where the time goes:
time: 493 us; the launch traced here: 485 us
  waiting for transfers between devices  304 us (62%)
  local copies, waits for them, and re-layouts  62.2 us (13%)
  matrix products  44.9 us (9%)
  other arithmetic  32.7 us (7%)
  starting transfers between devices  26.5 us (5%)
  between operations  14.7 us (3%)
    psum x1, waiting for transfers between devices, body(): lax.psum(shortened(partial_weights), ('tok', 'seq'))  128 us
    psum x2, waiting for transfers between devices, body(): summed_inner = lax.psum(partial_inner, 'tok')  113 us
    psum x1, waiting for transfers between devices, body(): summed_new = lax.psum(partial_new, 'tok')  35.5 us
    unnamed x91, local copies, waits for them, and re-layouts  31.4 us
    all_to_all x3, waiting for transfers between devices, side_by_side(): lax.all_to_all(both, axis, split_axis=split_dim, concat_axis=concat_dim,...  27.1 us
    all_to_all x3, starting transfers between devices, side_by_side(): lax.all_to_all(both, axis, split_axis=split_dim, concat_axis=concat_dim,...  19.5 us
    dot_general x9, matrix products, matmul_tn(): lax.dot_general(left.astype(jnp.bfloat16), right.astype(jnp.bfloat16), ((...  18.1 us
    dot_general x9, matrix products, matmul_nt(): lax.dot_general(left.astype(jnp.bfloat16), right.astype(jnp.bfloat16), ((...  17.5 us
  transfers between devices with their start and end apart: 8, of which 6 were waited for; matrix products, arithmetic and copies ran while one was open for 19% of the time, Pallas kernels for 0%

commit v1 on v0

v1 whole, which is shorter than its diff:
```python
import functools

import jax
import jax.numpy as jnp
from jax import lax
from jax.experimental import pallas as pl
from jax.experimental.pallas import tpu as pltpu
from jax.sharding import PartitionSpec as P

MESH = pl.DeviceIdType.MESH
EPS = 1e-06
BF = jnp.bfloat16
F32 = jnp.float32


def mm(a, b):
    return jnp.dot(a, b, preferred_element_type=F32)


def mm_tn(a, b):
    return lax.dot_general(a, b, (((0,), (0,)), ((), ())), preferred_element_type=F32)


def mm_nt(a, b):
    return lax.dot_general(a, b, (((1,), (1,)), ((), ())), preferred_element_type=F32)


def across(r, width):
    return jnp.concatenate([r] * (width // r.shape[-1]), axis=-1)


def kernel(T, H, *refs):
    (q, k, v, rates, w1, w2, w3, e) = refs[:8]
    (gq, gk, gv, grates, gf1, gf2, gf3) = refs[8:15]
    (kx, vx, qx, ex, wf, wb, wt, rmat) = refs[15:23]
    (hid, tgt, d1b, d3b, c1, c2, c3, c4) = refs[23:31]
    (dc1b, dc3b, gacc, gqb, gkb, gvb) = refs[31:37]
    (send_a, recv_a, send_b, recv_b, full, ush, dsh, sq_send, sq_recv, outf) = refs[37:47]
    (in_send, in_recv, w_sem, a_send, a_recv, b_send, b_recv) = refs[47:54]
    (ag_send, ag_recv, fw_send, fw_recv, s_send, s_recv, o_send, o_recv, f_sem) = refs[54:63]

    X, Y = T // 2, H // 2
    TB, PD = kx.shape[1], kx.shape[2]
    SH = full.shape[3]
    CH = 2 * TB
    t, h, s = lax.axis_index("tok"), lax.axis_index("head"), lax.axis_index("seq")
    x, c = t // 2, lax.rem(t, 2)
    y, zh = h // 2, lax.rem(h, 2)

    def head_of(dy, dz):
        return lax.rem(y + dy, Y) * 2 + lax.rem(zh + dz, 2)

    def tok_of(d):
        return lax.rem(x + d, X) * 2 + c

    partner = {"tok": x * 2 + 1 - c}
    other_seq = {"seq": 1 - s}

    def order(i):
        return i + (i // 2) * (5 - 2 * i) if Y == 4 else i

    def remote(src, dst, ss, rs, dev):
        cp = pltpu.make_async_remote_copy(
            src_ref=src, dst_ref=dst, send_sem=ss, recv_sem=rs, device_id=dev, device_id_type=MESH
        )
        return cp

    def arrived(ref, sem):
        pltpu.make_async_copy(ref, ref, sem).wait()

    barrier = pltpu.get_barrier_semaphore()
    greeted = [{"head": head_of(i // 2, i % 2)} for i in range(1, H)]
    greeted += [{"tok": tok_of(d)} for d in range(1, X)]
    greeted += [partner, other_seq]
    for dev in greeted:
        pl.semaphore_signal(barrier, inc=1, device_id=dev, device_id_type=MESH)
    pl.semaphore_wait(barrier, len(greeted))

    for n, (src, dst) in enumerate(((k, kx), (v, vx), (q, qx), (e, ex))):
        for i in range(1, H):
            dy, dz = i // 2, i % 2
            back = ((Y - dy) % Y) * 2 + dz
            peer = head_of(dy, dz)
            remote(
                src.at[0, :, pl.ds(pl.multiple_of(peer * PD, PD), PD)],
                dst.at[back],
                in_send.at[n, i],
                in_recv.at[n, back],
                {"head": peer},
            ).start()
        pltpu.make_async_copy(
            src.at[0, :, pl.ds(pl.multiple_of(h * PD, PD), PD)], dst.at[0], in_recv.at[n, 0]
        ).start()
    for j, w in enumerate((w1, w2, w3)):
        pltpu.make_async_copy(w.at[0], wf.at[j], w_sem.at[j]).start()

    @pl.loop(0, 3)
    def _(j):
        arrived(wf.at[j], w_sem.at[j])
        wb[j] = wf[j].astype(BF)
        wt[j] = wf[j, :, pl.ds(pl.multiple_of(x * 2 * SH, 2 * SH), 2 * SH)].T.reshape(2, SH, PD)

    @pl.loop(0, H)
    def _(i):
        p = head_of(i // 2, lax.rem(i, 2))
        r = rates[0, :, pl.ds(pl.multiple_of(p * TB, TB), TB)]
        rmat[i] = jnp.broadcast_to(r, (TB, TB)).T

    gacc[...] = jnp.zeros_like(gacc)

    def put(ref, dy, val):
        ref[pl.ds(dy * 2, 2)] = val.reshape(2, TB, PD)

    def get(ref, dy):
        return ref[pl.ds(dy * 2, 2)].reshape(CH, PD)

    @pl.loop(0, Y)
    def _(i):
        dy = order(i)
        for dz in range(2):
            arrived(kx.at[dy * 2 + dz], in_recv.at[0, dy * 2 + dz])
        kk = get(kx, dy)
        a1 = mm(kk, wb[0])
        a3 = mm(kk, wb[2])
        sg = jax.nn.sigmoid(a1)
        om = 1.0 - sg
        swish = a1 * sg
        slope = sg * (1.0 + a1 * om)
        slope2 = sg * om * (2.0 + a1 * (om - sg))
        hb = (swish * a3).astype(BF)
        gate = a3 * slope
        put(hid, dy, hb)
        put(c1, dy, gate)
        put(c2, dy, swish)
        for dz in range(2):
            arrived(vx.at[dy * 2 + dz], in_recv.at[1, dy * 2 + dz])
        rr = across(get_r(rmat, dy, CH, TB), PD)
        tb = (-rr * get(vx, dy).astype(F32)).astype(BF)
        put(tgt, dy, tb)
        b = mm_nt(tb, wb[1])
        db1 = (b * gate).astype(BF)
        db3 = (b * swish).astype(BF)
        put(d1b, dy, db1)
        put(d3b, dy, db3)
        put(c3, dy, b * slope)
        put(c4, dy, b * (a3 * slope2))
        gacc[1] += mm_tn(tb, hb)
        gacc[0] += mm_tn(db1, kk)
        gacc[2] += mm_tn(db3, kk)

    def scatter_start(n, j):
        g = gacc.at[j].reshape(X, 2, SH, PD)
        send_a[n, j] = g[:, 1 - c].astype(BF)
        remote(send_a.at[n, j], recv_a.at[n, j], a_send.at[n, j], a_recv.at[n, j], partner).start()

    def scatter_mid(n, j):
        g = gacc.at[j].reshape(X, 2, SH, PD)
        arrived(recv_a.at[n, j], a_recv.at[n, j])
        for d in range(1, X):
            xo = lax.rem(x + d, X)
            send_b[n, j, d - 1] = (g[xo, c] + recv_a[n, j, xo].astype(F32)).astype(BF)
            remote(
                send_b.at[n, j, d - 1],
                recv_b.at[n, j, d - 1],
                b_send.at[n, j, d - 1],
                b_recv.at[n, j, d - 1],
                {"tok": tok_of(d)},
            ).start()

    def scatter_end(n, j):
        g = gacc.at[j].reshape(X, 2, SH, PD)
        total = g[x, c] + recv_a[n, j, x].astype(F32)
        for d in range(1, X):
            arrived(recv_b.at[n, j, d - 1], b_recv.at[n, j, d - 1])
            total += recv_b[n, j, d - 1].astype(F32)
        return total

    def gather_start(n, j, val):
        full[n, j, t] = val.astype(BF)
        for d in range(1, X):
            remote(
                full.at[n, j, t],
                full.at[n, j, t],
                ag_send.at[n, j, d - 1],
                ag_recv.at[n, j, d - 1],
                {"tok": tok_of(d)},
            ).start()
        remote(full.at[n, j, t], full.at[n, j, t], fw_send.at[n, j, 0], fw_recv.at[n, j, 0], partner).start()

    def gather_mid(n, j):
        for d in range(1, X):
            src = full.at[n, j, tok_of(X - d)]
            arrived(src, ag_recv.at[n, j, d - 1])
            remote(src, src, fw_send.at[n, j, d], fw_recv.at[n, j, d], partner).start()

    def gather_end(n, j):
        for d in range(X):
            src = full.at[n, j, lax.rem(x + X - d, X) * 2 + 1 - c]
            arrived(src, fw_recv.at[n, j, d])

    JS = (1, 0, 2)
    for j in JS:
        scatter_start(0, j)
    for j in JS:
        scatter_mid(0, j)
    for j in JS:
        w = wt[j, c]
        u = w - scatter_end(0, j)
        rn = jnp.sqrt(jnp.sum(w * w, axis=1, keepdims=True) + EPS)
        un = jnp.sqrt(jnp.sum(u * u, axis=1, keepdims=True) + EPS)
        ush[j] = u
        gather_start(0, j, u * (rn / un))
    for j in JS:
        gather_mid(0, j)
    gacc[...] = jnp.zeros_like(gacc)
    for j in JS:
        gather_end(0, j)

    def whole(n, j):
        return full[n, j].reshape(PD, PD)

    @pl.loop(0, Y)
    def _(i):
        dy = order(i)
        for dz in range(2):
            arrived(qx.at[dy * 2 + dz], in_recv.at[2, dy * 2 + dz])
            arrived(ex.at[dy * 2 + dz], in_recv.at[3, dy * 2 + dz])
        qq = get(qx, dy)
        ee = get(ex, dy)
        p1 = mm_nt(qq, whole(0, 0))
        p3 = mm_nt(qq, whole(0, 2))
        sg = jax.nn.sigmoid(p1)
        swish = p1 * sg
        slope = sg * (1.0 + p1 * (1.0 - sg))
        mb = (swish * p3).astype(BF)
        dm = mm(ee, whole(0, 1))
        x1 = (dm * p3 * slope).astype(BF)
        x3 = (dm * swish).astype(BF)
        put(dc1b, dy, x1)
        put(dc3b, dy, x3)
        gacc[1] += mm_tn(ee, mb)
        gacc[0] += mm_tn(x1, qq)
        gacc[2] += mm_tn(x3, qq)

    for j in JS:
        scatter_start(1, j)
    for j in JS:
        scatter_mid(1, j)

    def send_back(n, src, dst, dy):
        for dz in range(2):
            i = dy * 2 + dz
            peer = head_of(dy, dz)
            mine = dst.at[0, :, pl.ds(pl.multiple_of(h * PD, PD), PD)]
            cp = remote(src.at[i], mine, o_send.at[n, i], o_recv.at[n, lax.rem(Y - dy, Y) * 2 + dz], {"head": peer})
            if dz:
                cp.start()
            else:
                pl.when(dy != 0)(cp.start)
                pl.when(dy == 0)(pltpu.make_async_copy(src.at[i], mine, o_recv.at[n, 0]).start)

    @pl.loop(0, Y)
    def _(i):
        dy = order(i)
        g = mm(get(dc1b, dy), whole(0, 0)) + mm(get(dc3b, dy), whole(0, 2))
        put(gqb, dy, g.astype(BF))
        send_back(0, gqb, gq, dy)

    for j in JS:
        w = wt[j, c]
        u = ush[j]
        dnew = scatter_end(1, j)
        rn = jnp.sqrt(jnp.sum(w * w, axis=1, keepdims=True) + EPS)
        un = jnp.sqrt(jnp.sum(u * u, axis=1, keepdims=True) + EPS)
        moment = jnp.sum(dnew * u, axis=1, keepdims=True)
        factor = rn / un
        du = factor * dnew - u * (factor * moment / (un * un))
        dsh[j] = w * (moment / (un * rn)) + du
        gather_start(1, j, -du)
    for j in JS:
        gather_mid(1, j)
    gacc[...] = jnp.zeros_like(gacc)
    for j in JS:
        gather_end(1, j)

    @pl.loop(0, Y)
    def _(i):
        dy = order(i)
        kk = get(kx, dy)
        tb = get(tgt, dy)
        hb = get(hid, dy)
        gate, swish, bs, bc = get(c1, dy), get(c2, dy), get(c3, dy), get(c4, dy)
        dh = mm(tb, whole(1, 1))
        dd1 = mm_nt(kk, whole(1, 0))
        dd3 = mm_nt(kk, whole(1, 2))
        dbb = (dd1 * gate + dd3 * swish).astype(BF)
        da3 = (dd1 * bs + dh * swish).astype(BF)
        da1 = (dd1 * bc + dd3 * bs + dh * gate).astype(BF)
        gk_new = (mm(get(d1b, dy), whole(1, 0)) + mm(get(d3b, dy), whole(1, 2))) + (
            mm_nt(da1, wb[0]) + mm_nt(da3, wb[2])
        )
        put(gkb, dy, gk_new.astype(BF))
        send_back(1, gkb, gk, dy)
        dt = mm_nt(hb, whole(1, 1)) + mm(dbb, wb[1])
        rr = across(get_r(rmat, dy, CH, TB), PD)
        put(gvb, dy, (-rr * dt).astype(BF))
        send_back(2, gvb, gv, dy)
        prod = get(vx, dy).astype(F32) * dt
        fold = prod[:, :TB]
        for m in range(1, PD // TB):
            fold += prod[:, m * TB : (m + 1) * TB]
        for dz in range(2):
            row = -jnp.sum(fold[dz * TB : (dz + 1) * TB].T, axis=0, keepdims=True)
            grates[0, :, pl.ds(pl.multiple_of(head_of(dy, dz) * TB, TB), TB)] = row
        gacc[1] += mm_tn(tb, dbb)
        gacc[0] += mm_tn(da1, kk)
        gacc[2] += mm_tn(da3, kk)

    for j in JS:
        scatter_start(2, j)
    for j in JS:
        scatter_mid(2, j)
    for j in JS:
        sq_send[j] = (scatter_end(2, j) + dsh[j]).astype(BF)
        remote(sq_send.at[j], sq_recv.at[j], s_send.at[j], s_recv.at[j], other_seq).start()
    for j in JS:
        arrived(sq_recv.at[j], s_recv.at[j])
        gather_start(2, j, sq_send[j].astype(F32) + sq_recv[j].astype(F32))
    for j in JS:
        gather_mid(2, j)
    outs = (gf1, gf2, gf3)
    for j in JS:
        gather_end(2, j)
        for m in range(X):
            part = full[2, j, 2 * m : 2 * m + 2].reshape(2 * SH, PD).astype(F32)
            outf[j, :, m * 2 * SH : (m + 1) * 2 * SH] = part.T
        pltpu.make_async_copy(outf.at[j], outs[j].at[0], f_sem.at[j]).start()

    for n, dst in enumerate((gq, gk, gv)):
        for i in range(H):
            mine = dst.at[0, :, pl.ds(pl.multiple_of(head_of(i // 2, i % 2) * PD, PD), PD)]
            arrived(mine, o_recv.at[n, i])
    for n, src in enumerate((gqb, gkb, gvb)):
        for i in range(1, H):
            arrived(src.at[i], o_send.at[n, i])
    for n, src in enumerate((kx, vx, qx, ex)):
        for i in range(1, H):
            arrived(src.at[i], in_send.at[n, i])
    for n in range(3):
        for j in range(3):
            arrived(send_a.at[n, j], a_send.at[n, j])
            for d in range(1, X):
                arrived(send_b.at[n, j, d - 1], b_send.at[n, j, d - 1])
                arrived(full.at[n, j, 0], ag_send.at[n, j, d - 1])
            for d in range(X):
                arrived(full.at[n, j, 0], fw_send.at[n, j, d])
    for j in range(3):
        arrived(sq_send.at[j], s_send.at[j])
        arrived(outf.at[j], f_sem.at[j])


def get_r(rmat, dy, rows, width):
    return rmat[pl.ds(dy * 2, 2)].reshape(rows, width)


def solution(mesh):
    T, H = mesh.shape["tok"], mesh.shape["head"]
    assert T % 2 == 0 and H % 2 == 0 and mesh.shape["seq"] == 2

    def body(queries, keys, values, rates, fast_one, fast_two, fast_three, grad_out):
        tb, d = queries.shape[1], queries.shape[2]
        pd = fast_one.shape[1]
        n = tb * H
        X = T // 2
        sh = pd // T
        assert d == pd * H and rates.shape[2] == n

        def vm(*shape, dtype=BF):
            return pltpu.VMEM(shape, dtype)

        dma = pltpu.SemaphoreType.DMA
        tok = lambda dtype=BF: vm(H, tb, pd, dtype=dtype)
        scratch = [
            tok(), tok(), tok(), tok(),
            vm(3, pd, pd, dtype=F32), vm(3, pd, pd), vm(3, 2, sh, pd, dtype=F32), vm(H, tb, tb, dtype=F32),
            tok(), tok(), tok(), tok(), tok(F32), tok(F32), tok(F32), tok(F32),
            tok(), tok(), vm(3, pd, pd, dtype=F32), tok(), tok(), tok(),
            vm(3, 3, X, sh, pd), vm(3, 3, X, sh, pd),
            vm(3, 3, max(X - 1, 1), sh, pd), vm(3, 3, max(X - 1, 1), sh, pd),
            vm(3, 3, T, sh, pd), vm(3, sh, pd, dtype=F32), vm(3, sh, pd, dtype=F32),
            vm(3, sh, pd), vm(3, sh, pd), vm(3, pd, pd, dtype=F32),
            dma((4, H)), dma((4, H)), dma((3,)), dma((3, 3)), dma((3, 3)),
            dma((3, 3, max(X - 1, 1))), dma((3, 3, max(X - 1, 1))),
            dma((3, 3, max(X - 1, 1))), dma((3, 3, max(X - 1, 1))),
            dma((3, 3, X)), dma((3, 3, X)), dma((3,)), dma((3,)), dma((3, H)), dma((3, H)), dma((3,)),
        ]
        anyspace = pl.BlockSpec(memory_space=pl.ANY)
        vmem = pl.BlockSpec(memory_space=pltpu.VMEM)
        shape = jax.ShapeDtypeStruct
        return pl.pallas_call(
            functools.partial(kernel, T, H),
            out_shape=(
                shape(queries.shape, BF),
                shape(queries.shape, BF),
                shape(queries.shape, BF),
                shape(rates.shape, F32),
                shape(fast_one.shape, F32),
                shape(fast_one.shape, F32),
                shape(fast_one.shape, F32),
            ),
            in_specs=[anyspace, anyspace, anyspace, vmem] + [anyspace] * 4,
            out_specs=(anyspace, anyspace, anyspace, vmem, anyspace, anyspace, anyspace),
            scratch_shapes=scratch,
            compiler_params=pltpu.CompilerParams(
                collective_id=0, has_side_effects=True, vmem_limit_bytes=62 * 1024 * 1024
            ),
            name="layer",
        )(queries, keys, values, rates, fast_one, fast_two, fast_three, grad_out)

    tokens = P("seq", ("tok", "head"), None)
    row = P("seq", "head", "tok")
    weight = P("head", None, None)
    return jax.shard_map(
        body,
        mesh=mesh,
        in_specs=(tokens, tokens, tokens, row, weight, weight, weight, tokens),
        out_specs=(tokens, tokens, tokens, row, weight, weight, weight),
        check_vma=False,
    )
```

time: 493 us -> 141 us (0.29); the launches traced: 485 us -> 140 us
  waiting for transfers between devices: 304 us -> 0 us
  Pallas kernels: 0 us -> 130 us
  local copies, waits for them, and re-layouts: 62.2 us -> 9.76 us
  matrix products: 44.9 us -> 0 us
  other arithmetic: 32.7 us -> 0 us
  starting transfers between devices: 26.5 us -> 0 us
  between operations: 14.7 us -> 0.66 us
    psum x4 -> x0, waiting for transfers between devices: 277 us -> none  [the longest x1 128 us: body(): lax.psum(shortened(partial_weights), ('tok', 'seq'))]
    pallas_call x0 -> x1, Pallas kernels: none -> 130 us  [body(): pl.pallas_call(functools.partial(kernel, T, H), out_shape=(shape(queries....]
    dot_general x26 -> x0, matrix products: 44.9 us -> none  [the longest x9 18.1 us: matmul_tn(): lax.dot_general(left.astype(jnp.bfloat16), right.astype(jnp.bfloat16), ((...]
    all_to_all x4 -> x0, waiting for transfers between devices: 27.1 us -> none  [the longest x3 27.1 us: side_by_side(): lax.all_to_all(both, axis, split_axis=split_dim, concat_axis=concat_dim,...]
    all_to_all x4 -> x0, starting transfers between devices: 26.1 us -> none  [the longest x3 19.5 us: side_by_side(): lax.all_to_all(both, axis, split_axis=split_dim, concat_axis=concat_dim,...]
    unnamed x91 -> x19, local copies, waits for them, and re-layouts: 31.4 us -> 9.76 us
    split x9 -> x0, local copies, waits for them, and re-layouts: 13.2 us -> none  [side_by_side(): jnp.split(lax.all_to_all(both, axis, split_axis=split_dim, concat_axis=co...]
    unnamed x1 -> x0, other arithmetic: 9 us -> none
  transfers between devices with their start and end apart: 8 -> 0, of which waited for: 6 -> 0; matrix products, arithmetic and copies ran while one was open for 19% -> 0% of each run, Pallas kernels for 0% -> 0%
where the time goes in v1:
time: 141 us; the launch traced here: 140 us
  Pallas kernels  130 us (92%)
  local copies, waits for them, and re-layouts  9.76 us (7%)
    pallas_call x1, Pallas kernels, body(): pl.pallas_call(functools.partial(kernel, T, H), out_shape=(shape(queries....  130 us
    unnamed x19, local copies, waits for them, and re-layouts  9.76 us

profile of v1, /device:TPU:1, one launch (start us, length us, event | category | flops | bytes accessed | tf_op | source)
XLA Modules:
  0.0 140.4 jit_solution(12462091737370393639)
XLA Ops:
  0.6 129.9 %layer.1 = (bf16[1,128,4096]{2,1,0:T(8,128)(2,1)}, bf16[1,128,4096]{2,1,0:T(8,128)(2,1)}, bf16[1,128,4096]{2,1,0:T(8,128)(2,1)}, f32[1,1,1024]{2,1,0:T(1,128)}, ...) custom-call(bf16[1,128,4096]{2,1,0:T(8,128)(2,1)} %refs_0_.1, ...), custom_call_target="tpu_custom_call" | custom-call | tf_op jit(solution)/shard_map/layer/pallas_call | solution.py:400
  130.6 0.0 copy-start.4
  130.6 2.4 %copy.22 = bf16[1,128,4096]{2,1,0:T(8,128)(2,1)} copy(bf16[1,128,4096]{2,1,0:T(8,128)(2,1)} %get-tuple-element.14) | data formatting | bytes 2097152
  133.0 0.0 copy-done.4
  133.0 0.0 copy-start.3
  133.0 1.0 copy.23
  133.9 0.6 copy-done.3
  134.6 0.0 copy-start.5
  134.6 0.0 copy-start.2
  134.6 1.0 copy.24
  135.5 0.0 copy-done.5
  135.6 0.6 copy.25
  136.1 0.0 copy-done.2
  136.2 0.0 copy-start.1
  136.2 1.0 copy.26
  137.2 0.6 copy-done.1
  137.8 0.0 copy-start
  137.8 1.0 copy.27
  138.8 0.6 copy-done
  139.4 1.0 copy.28
Async XLA Ops:
  130.6 2.4 %copy-start.4 = (bf16[1,128,4096]{2,1,0:T(8,128)(2,1)S(1)}, bf16[1,128,4096]{2,1,0:T(8,128)(2,1)}, u32[]{:S(2)}) copy-start(bf16[1,128,4096]{2,1,0:T(8,128)(2,1)} %get-tuple-element.15) | copy-start | bytes 3145732
  133.0 1.6 %copy-start.3 = (bf16[1,128,4096]{2,1,0:T(8,128)(2,1)S(1)}, bf16[1,128,4096]{2,1,0:T(8,128)(2,1)}, u32[]{:S(2)}) copy-start(bf16[1,128,4096]{2,1,0:T(8,128)(2,1)} %get-tuple-element.16) | copy-start | bytes 3145732
  134.6 1.0 copy-start.5
  134.6 1.6 %copy-start.2 = (f32[1,512,512]{2,1,0:T(8,128)S(1)}, f32[1,512,512]{2,1,0:T(8,128)}, u32[]{:S(2)}) copy-start(f32[1,512,512]{2,1,0:T(8,128)} %get-tuple-element.18) | copy-start | bytes 3145732
  136.2 1.6 %copy-start.1 = (f32[1,512,512]{2,1,0:T(8,128)S(1)}, f32[1,512,512]{2,1,0:T(8,128)}, u32[]{:S(2)}) copy-start(f32[1,512,512]{2,1,0:T(8,128)} %get-tuple-element.19) | copy-start | bytes 3145732
  137.8 1.6 %copy-start = (f32[1,512,512]{2,1,0:T(8,128)S(1)}, f32[1,512,512]{2,1,0:T(8,128)}, u32[]{:S(2)}) copy-start(f32[1,512,512]{2,1,0:T(8,128)} %get-tuple-element.20) | copy-start | bytes 3145732

commit v2 on v1

v2 whole, which is shorter than its diff:
```python
import functools

import jax
import jax.numpy as jnp
from jax import lax
from jax.experimental import pallas as pl
from jax.experimental.pallas import tpu as pltpu
from jax.sharding import PartitionSpec as P

MESH = pl.DeviceIdType.MESH
EPS = 1e-06
VLIM = 56 * 1024 * 1024
NC = 4
BF = jnp.bfloat16
F32 = jnp.float32


def mm(a, b):
    return jnp.dot(a, b, preferred_element_type=F32)


def mm_tn(a, b):
    return lax.dot_general(a, b, (((0,), (0,)), ((), ())), preferred_element_type=F32)


def mm_nt(a, b):
    return lax.dot_general(a, b, (((1,), (1,)), ((), ())), preferred_element_type=F32)


def across(r, width):
    return jnp.concatenate([r] * (width // r.shape[-1]), axis=-1)


def kernel(T, H, *refs):
    (q, k, v, rates, w1, w2, w3, e) = refs[:8]
    (gq, gk, gv, grates, gf1, gf2, gf3) = refs[8:15]
    (kx, vx, qx, ex, wf, wb, wt, rmat) = refs[15:23]
    (hid, tgt, d1b, d3b, c1, c2, c3, c4) = refs[23:31]
    (dc1b, dc3b, dbb, gacc, gqb, gkb, gvb, rsum) = refs[31:39]
    (send_a, recv_a, send_1, recv_1, send_2, recv_2, full, ush, dsh, sq_send, sq_recv) = refs[39:50]
    (in_send, in_recv, w_sem, as_sem, ar_sem, s1_sem, r1_sem, s2_sem, r2_sem) = refs[50:59]
    (gs1_sem, gr1_sem, gs2_sem, gr2_sem, fs_sem, fr_sem, qs_sem, qr_sem, o_send, o_recv) = refs[59:69]

    X, Y = T // 2, H // 2
    TB, PD = kx.shape[1], kx.shape[2]
    NC = in_send.shape[1]
    CR = TB // NC
    SH = full.shape[3]
    CH = H * CR
    t, h, s = lax.axis_index("tok"), lax.axis_index("head"), lax.axis_index("seq")
    x, c = t // 2, lax.rem(t, 2)
    y, zh = h // 2, lax.rem(h, 2)

    def head_of(dy, dz):
        return lax.rem(y + dy, Y) * 2 + lax.rem(zh + dz, 2)

    na = x + 1 - 2 * lax.rem(x, 2)
    nb = lax.rem(x + 3 + 2 * lax.rem(x, 2), 4)
    opp = lax.rem(x + 2, 4)
    SIDE = ((0, na), (1, nb))

    partner = {"tok": x * 2 + 1 - c}
    other_seq = {"seq": 1 - s}

    def part(n):
        return pl.ds(pl.multiple_of(n * CR, CR), CR)

    def remote(src, dst, ss, rs, dev):
        cp = pltpu.make_async_remote_copy(
            src_ref=src, dst_ref=dst, send_sem=ss, recv_sem=rs, device_id=dev, device_id_type=MESH
        )
        return cp

    def arrived(ref, sem):
        pltpu.make_async_copy(ref, ref, sem).wait()

    barrier = pltpu.get_barrier_semaphore()
    greeted = [{"head": head_of(i // 2, i % 2)} for i in range(1, H)]
    greeted += [{"tok": na * 2 + c}, {"tok": nb * 2 + c}, partner, other_seq]
    for dev in greeted:
        pl.semaphore_signal(barrier, inc=1, device_id=dev, device_id_type=MESH)
    pl.semaphore_wait(barrier, len(greeted))

    for a in (0, 2):

        @pl.loop(0, NC)
        def _(m):
            for n in (a, a + 1):
                src, dst = ((k, kx), (v, vx), (q, qx), (e, ex))[n]
                for i in range(H):
                    dy, dz = i // 2, i % 2
                    back = ((Y - dy) % Y) * 2 + dz
                    peer = head_of(dy, dz)
                    here = src.at[0, part(m), pl.ds(pl.multiple_of(peer * PD, PD), PD)]
                    there = dst.at[back, part(m)]
                    if i:
                        remote(here, there, in_send.at[n, m], in_recv.at[n, m], {"head": peer}).start()
                    else:
                        pltpu.make_async_copy(here, there, in_recv.at[n, m]).start()

    for j, w in enumerate((w1, w2, w3)):
        pltpu.make_async_copy(w.at[0], wf.at[j], w_sem.at[j]).start()

    @pl.loop(0, 3)
    def _(j):
        arrived(wf.at[j], w_sem.at[j])
        wb[j] = wf[j].astype(BF)
        wt[j] = wf[j, :, pl.ds(pl.multiple_of(x * 2 * SH, 2 * SH), 2 * SH)].T.reshape(2, SH, PD)

    @pl.loop(0, H)
    def _(i):
        p = head_of(i // 2, lax.rem(i, 2))
        r = rates[0, :, pl.ds(pl.multiple_of(p * TB, TB), TB)]
        rmat[i] = jnp.broadcast_to(r, (TB, TB)).T

    gacc[...] = jnp.zeros_like(gacc)

    def put(ref, m, val):
        ref[:, part(m)] = val.reshape(H, CR, val.shape[-1])

    def get(ref, m):
        return ref[:, part(m)].reshape(CH, ref.shape[-1])

    @pl.loop(0, NC)
    def _(m):
        arrived(kx.at[:, part(m)], in_recv.at[0, m])
        kk = get(kx, m)
        a1 = mm(kk, wb[0])
        a3 = mm(kk, wb[2])
        sg = jax.nn.sigmoid(a1)
        om = 1.0 - sg
        swish = a1 * sg
        slope = sg * (1.0 + a1 * om)
        slope2 = sg * om * (2.0 + a1 * (om - sg))
        hb = (swish * a3).astype(BF)
        gate = a3 * slope
        put(hid, m, hb)
        put(c1, m, gate)
        put(c2, m, swish)
        arrived(vx.at[:, part(m)], in_recv.at[1, m])
        rr = across(get(rmat, m), PD)
        tb = (-rr * get(vx, m).astype(F32)).astype(BF)
        put(tgt, m, tb)
        b = mm_nt(tb, wb[1])
        db1 = (b * gate).astype(BF)
        db3 = (b * swish).astype(BF)
        put(d1b, m, db1)
        put(d3b, m, db3)
        put(c3, m, b * slope)
        put(c4, m, b * (a3 * slope2))
        gacc[1] += mm_tn(tb, hb)
        gacc[0] += mm_tn(db1, kk)
        gacc[2] += mm_tn(db3, kk)

    HF = SH // 2

    def rows(p):
        return pl.ds(p * HF, HF)

    def cores_start(n, j):
        g = gacc.at[j].reshape(X, 2, SH, PD)
        send_a[n, j] = g[:, 1 - c].astype(BF)
        remote(send_a.at[n, j], recv_a.at[n, j], as_sem.at[n, j], ar_sem.at[n, j], partner).start()

    def chip_sum(n, j, piece, p):
        g = gacc.at[j].reshape(X, 2, SH, PD)
        return g[piece, c, rows(p)] + recv_a[n, j, piece, rows(p)].astype(F32)

    def halve_start(n, j):
        arrived(recv_a.at[n, j], ar_sem.at[n, j])
        for p, near in SIDE:
            for m, piece in enumerate((near, opp)):
                send_1[n, j, p, m] = chip_sum(n, j, piece, p).astype(BF)
            remote(
                send_1.at[n, j, p], recv_1.at[n, j, p], s1_sem.at[n, j, p], r1_sem.at[n, j, p], {"tok": near * 2 + c}
            ).start()

    def halve_again(n, j):
        for p, near in ((0, nb), (1, na)):
            arrived(recv_1.at[n, j, p], r1_sem.at[n, j, p])
            send_2[n, j, p] = (chip_sum(n, j, near, p) + recv_1[n, j, p, 1].astype(F32)).astype(BF)
            remote(
                send_2.at[n, j, p], recv_2.at[n, j, p], s2_sem.at[n, j, p], r2_sem.at[n, j, p], {"tok": near * 2 + c}
            ).start()

    def scatter_end(n, j):
        parts = []
        for p in range(2):
            arrived(recv_2.at[n, j, p], r2_sem.at[n, j, p])
            parts.append(chip_sum(n, j, x, p) + recv_1[n, j, p, 0].astype(F32) + recv_2[n, j, p].astype(F32))
        return jnp.concatenate(parts, axis=0)

    def send_rows(ref, ss, rs, dev):
        remote(ref, ref, ss, rs, dev).start()

    def gather_start(n, j, val):
        full[n, j, t] = val.astype(BF)
        mine = full.at[n, j, t]
        for p, near in SIDE:
            send_rows(mine, gs1_sem.at[n, j, p], gr1_sem.at[n, j, p], {"tok": near * 2 + c})
        send_rows(mine, fs_sem.at[n, j, 0], fr_sem.at[n, j, 0], partner)

    def gather_mid(n, j):
        for p, near in SIDE:
            got = full.at[n, j, near * 2 + c]
            arrived(got, gr1_sem.at[n, j, p])
            q, far = 1 - p, (nb, na)[p]
            send_rows(got.at[rows(q)], gs2_sem.at[n, j, q], gr2_sem.at[n, j, q], {"tok": far * 2 + c})
            send_rows(got, fs_sem.at[n, j, 1 + p], fr_sem.at[n, j, 1 + p], partner)

    def gather_far(n, j):
        for p in range(2):
            got = full.at[n, j, opp * 2 + c, rows(p)]
            arrived(got, gr2_sem.at[n, j, p])
            send_rows(got, fs_sem.at[n, j, 3 + p], fr_sem.at[n, j, 3 + p], partner)

    def gather_end(n, j):
        for m, piece in enumerate((x, na, nb)):
            arrived(full.at[n, j, piece * 2 + 1 - c], fr_sem.at[n, j, m])
        for p in range(2):
            arrived(full.at[n, j, opp * 2 + 1 - c, rows(p)], fr_sem.at[n, j, 3 + p])

    JS = (1, 0, 2)

    def each(step, n):
        for j in JS:
            step(n, j)

    each(cores_start, 0)
    each(halve_start, 0)
    each(halve_again, 0)
    for j in JS:
        w = wt[j, c]
        u = w - scatter_end(0, j)
        rn = jnp.sqrt(jnp.sum(w * w, axis=1, keepdims=True) + EPS)
        un = jnp.sqrt(jnp.sum(u * u, axis=1, keepdims=True) + EPS)
        ush[j] = u
        gather_start(0, j, u * (rn / un))
    gacc[...] = jnp.zeros_like(gacc)
    each(gather_mid, 0)
    each(gather_far, 0)
    each(gather_end, 0)

    def whole(n, j):
        return full[n, j].reshape(PD, PD)

    @pl.loop(0, NC)
    def _(m):
        arrived(qx.at[:, part(m)], in_recv.at[2, m])
        arrived(ex.at[:, part(m)], in_recv.at[3, m])
        qq = get(qx, m)
        ee = get(ex, m)
        p1 = mm_nt(qq, whole(0, 0))
        p3 = mm_nt(qq, whole(0, 2))
        sg = jax.nn.sigmoid(p1)
        swish = p1 * sg
        slope = sg * (1.0 + p1 * (1.0 - sg))
        mb = (swish * p3).astype(BF)
        dm = mm(ee, whole(0, 1))
        x1 = (dm * p3 * slope).astype(BF)
        x3 = (dm * swish).astype(BF)
        put(dc1b, m, x1)
        put(dc3b, m, x3)
        gacc[1] += mm_tn(ee, mb)
        gacc[0] += mm_tn(x1, qq)
        gacc[2] += mm_tn(x3, qq)

    each(cores_start, 1)
    each(halve_start, 1)

    def send_back(n, src, dst, m, which=(0, 1)):
        for i in range(H):
            dy, dz = i // 2, i % 2
            if dz in which:
                here = src.at[i, part(m)]
                there = dst.at[0, part(m), pl.ds(pl.multiple_of(h * PD, PD), PD)]
                if i:
                    remote(here, there, o_send.at[n, m], o_recv.at[n, m], {"head": head_of(dy, dz)}).start()
                else:
                    pltpu.make_async_copy(here, there, o_recv.at[n, m]).start()

    @pl.loop(0, NC)
    def _(m):
        g = mm(get(dc1b, m), whole(0, 0)) + mm(get(dc3b, m), whole(0, 2))
        put(gqb, m, g.astype(BF))
        send_back(0, gqb, gq, m)

    each(halve_again, 1)
    for j in JS:
        w = wt[j, c]
        u = ush[j]
        dnew = scatter_end(1, j)
        rn = jnp.sqrt(jnp.sum(w * w, axis=1, keepdims=True) + EPS)
        un = jnp.sqrt(jnp.sum(u * u, axis=1, keepdims=True) + EPS)
        moment = jnp.sum(dnew * u, axis=1, keepdims=True)
        factor = rn / un
        du = factor * dnew - u * (factor * moment / (un * un))
        dsh[j] = w * (moment / (un * rn)) + du
        gather_start(1, j, -du)
    each(gather_mid, 1)
    each(gather_far, 1)
    each(gather_end, 1)

    @pl.loop(0, NC)
    def _(m):
        kk = get(kx, m)
        tb = get(tgt, m)
        hb = get(hid, m)
        gate, swish, bs, bc = get(c1, m), get(c2, m), get(c3, m), get(c4, m)
        dh = mm(tb, whole(1, 1))
        dd1 = mm_nt(kk, whole(1, 0))
        dd3 = mm_nt(kk, whole(1, 2))
        db = (dd1 * gate + dd3 * swish).astype(BF)
        put(dbb, m, db)
        put(dc3b, m, (dd1 * bs + dh * swish).astype(BF))
        put(dc1b, m, (dd1 * bc + dd3 * bs + dh * gate).astype(BF))
        dt = mm_nt(hb, whole(1, 1)) + mm(db, wb[1])
        rr = across(get(rmat, m), PD)
        put(gvb, m, (-rr * dt).astype(BF))
        send_back(2, gvb, gv, m)
        prod = get(vx, m).astype(F32) * dt
        fold = prod[:, :TB]
        for b in range(1, PD // TB):
            fold += prod[:, b * TB : (b + 1) * TB]
        put(rsum, m, fold)

    for j, (left, right) in ((1, (tgt, dbb)), (0, (dc1b, kx)), (2, (dc3b, kx))):
        gacc[j] = mm_tn(left[...].reshape(H * TB, PD), right[...].reshape(H * TB, PD))
        cores_start(2, j)
    each(halve_start, 2)

    @pl.loop(0, NC)
    def _(m):
        g = (mm(get(d1b, m), whole(1, 0)) + mm(get(d3b, m), whole(1, 2))) + (
            mm_nt(get(dc1b, m), wb[0]) + mm_nt(get(dc3b, m), wb[2])
        )
        put(gkb, m, g.astype(BF))
        send_back(1, gkb, gk, m, (0,))

    each(halve_again, 2)
    for j in JS:
        sq_send[j] = (scatter_end(2, j) + dsh[j]).astype(BF)
        remote(sq_send.at[j], sq_recv.at[j], qs_sem.at[j], qr_sem.at[j], other_seq).start()

    @pl.loop(0, NC)
    def _(m):
        send_back(1, gkb, gk, m, (1,))

    @pl.loop(0, H)
    def _(i):
        p = head_of(i // 2, lax.rem(i, 2))
        grates[0, :, pl.ds(pl.multiple_of(p * TB, TB), TB)] = -jnp.sum(rsum[i].T, axis=0, keepdims=True)

    for j in JS:
        arrived(sq_recv.at[j], qr_sem.at[j])
        gather_start(2, j, sq_send[j].astype(F32) + sq_recv[j].astype(F32))
    each(gather_mid, 2)
    each(gather_far, 2)
    outs = (gf1, gf2, gf3)
    for j in JS:
        gather_end(2, j)
        for b in range(X):
            pair = full[2, j, 2 * b : 2 * b + 2].reshape(2 * SH, PD).astype(F32)
            outs[j][0, :, b * 2 * SH : (b + 1) * 2 * SH] = pair.T

    @pl.loop(0, NC)
    def _(m):
        for n, dst in enumerate((gq, gk, gv)):
            arrived(dst.at[0, part(m)], o_recv.at[n, m])
        for n, src in enumerate((gqb, gkb, gvb)):
            arrived(src.at[pl.ds(1, H - 1), part(m)], o_send.at[n, m])
        for n, src in enumerate((kx, vx, qx, ex)):
            arrived(src.at[pl.ds(1, H - 1), part(m)], in_send.at[n, m])

    for n in range(3):
        for j in range(3):
            arrived(send_a.at[n, j], as_sem.at[n, j])
            for p in range(2):
                arrived(send_1.at[n, j, p], s1_sem.at[n, j, p])
                arrived(send_2.at[n, j, p], s2_sem.at[n, j, p])
                arrived(full.at[n, j, 0], gs1_sem.at[n, j, p])
                arrived(full.at[n, j, 0, rows(p)], gs2_sem.at[n, j, p])
                arrived(full.at[n, j, 0, rows(p)], fs_sem.at[n, j, 3 + p])
            for m in range(3):
                arrived(full.at[n, j, 0], fs_sem.at[n, j, m])
    for j in range(3):
        arrived(sq_send.at[j], qs_sem.at[j])


def put_out(*refs):
    n = len(refs) // 2
    copies = [pltpu.make_async_copy(refs[i], refs[n + i], refs[-1].at[i]) for i in range(n)]
    for cp in copies:
        cp.start()
    for cp in copies:
        cp.wait()


def solution(mesh):
    T, H = mesh.shape["tok"], mesh.shape["head"]
    assert T == 8 and H % 2 == 0 and mesh.shape["seq"] == 2

    def body(queries, keys, values, rates, fast_one, fast_two, fast_three, grad_out):
        tb, d = queries.shape[1], queries.shape[2]
        pd = fast_one.shape[1]
        n = tb * H
        X = T // 2
        sh = pd // T
        assert d == pd * H and rates.shape[2] == n

        def vm(*shape, dtype=BF):
            return pltpu.VMEM(shape, dtype)

        dma = pltpu.SemaphoreType.DMA
        tok = lambda dtype=BF: vm(H, tb, pd, dtype=dtype)
        scratch = [
            tok(), tok(), tok(), tok(),
            vm(3, pd, pd, dtype=F32), vm(3, pd, pd), vm(3, 2, sh, pd, dtype=F32), vm(H, tb, tb, dtype=F32),
            tok(), tok(), tok(), tok(), tok(F32), tok(F32), tok(F32), tok(F32),
            tok(), tok(), tok(), vm(3, pd, pd, dtype=F32), tok(), tok(), tok(), vm(H, tb, tb, dtype=F32),
            vm(3, 3, X, sh, pd), vm(3, 3, X, sh, pd),
            vm(3, 3, 2, 2, sh // 2, pd), vm(3, 3, 2, 2, sh // 2, pd),
            vm(3, 3, 2, sh // 2, pd), vm(3, 3, 2, sh // 2, pd),
            vm(3, 3, T, sh, pd), vm(3, sh, pd, dtype=F32), vm(3, sh, pd, dtype=F32),
            vm(3, sh, pd), vm(3, sh, pd),
            dma((4, NC)), dma((4, NC)), dma((3,)), dma((3, 3)), dma((3, 3)),
            dma((3, 3, 2)), dma((3, 3, 2)), dma((3, 3, 2)), dma((3, 3, 2)),
            dma((3, 3, 2)), dma((3, 3, 2)), dma((3, 3, 2)), dma((3, 3, 2)),
            dma((3, 3, 5)), dma((3, 3, 5)), dma((3,)), dma((3,)), dma((3, NC)), dma((3, NC)),
        ]
        anyspace = pl.BlockSpec(memory_space=pl.ANY)
        vmem = pl.BlockSpec(memory_space=pltpu.VMEM)
        kinds = [(queries.shape, BF)] * 3 + [(rates.shape, F32)] + [(fast_one.shape, F32)] * 3
        held = pl.pallas_call(
            functools.partial(kernel, T, H),
            out_shape=tuple(pltpu.VMEM(a, b) for a, b in kinds),
            in_specs=[anyspace, anyspace, anyspace, vmem] + [anyspace] * 4,
            out_specs=(vmem,) * 7,
            scratch_shapes=scratch,
            compiler_params=pltpu.CompilerParams(
                collective_id=0, has_side_effects=True, vmem_limit_bytes=VLIM
            ),
            name="layer",
        )(queries, keys, values, rates, fast_one, fast_two, fast_three, grad_out)
        held = [pltpu.with_memory_space_constraint(a, pltpu.VMEM) for a in held]
        return pl.pallas_call(
            put_out,
            out_shape=tuple(jax.ShapeDtypeStruct(a, b) for a, b in kinds),
            in_specs=[vmem] * 7,
            out_specs=(anyspace,) * 7,
            scratch_shapes=[dma((7,))],
            compiler_params=pltpu.CompilerParams(vmem_limit_bytes=1024 * 1024),
            name="out",
        )(*held)

    tokens = P("seq", ("tok", "head"), None)
    row = P("seq", "head", "tok")
    weight = P("head", None, None)
    return jax.shard_map(
        body,
        mesh=mesh,
        in_specs=(tokens, tokens, tokens, row, weight, weight, weight, tokens),
        out_specs=(tokens, tokens, tokens, row, weight, weight, weight),
        check_vma=False,
    )
```

time: 141 us -> 124 us (0.88)
  local copies, waits for them, and re-layouts: 9.76 us -> 0 us
  Pallas kernels: 130 us -> 123 us
    unnamed x19 -> x0, local copies, waits for them, and re-layouts: 9.76 us -> none
    pallas_call x1 -> x2, Pallas kernels: 130 us -> 123 us  [the longest x1 120 us: body(): pl.pallas_call(functools.partial(kernel, T, H), out_shape=tuple((pltpu.VM...]
where the time goes in v2:
time: 124 us
  Pallas kernels  123 us (99%)
    pallas_call x1, Pallas kernels, body(): pl.pallas_call(functools.partial(kernel, T, H), out_shape=tuple((pltpu.VM...  120 us
    pallas_call x1, Pallas kernels, body(): pl.pallas_call(put_out, out_shape=tuple((jax.ShapeDtypeStruct(a, b) for a...  2.74 us

profile of v2, /device:TPU:1, one launch (start us, length us, event | category | flops | bytes accessed | tf_op | source)
XLA Modules:
  0.0 123.6 jit_solution(10717777660246501957)
XLA Ops:
  0.6 120.2 %layer.1 = (bf16[1,128,4096]{2,1,0:T(8,128)(2,1)S(1)}, bf16[1,128,4096]{2,1,0:T(8,128)(2,1)S(1)}, bf16[1,128,4096]{2,1,0:T(8,128)(2,1)S(1)}, f32[1,1,1024]{2,1,0...) custom-call(bf16[1,128,4096]{2,1,0:T(8,128)(2,1)} %refs_0_.1, ...), custom_call_target="tpu_custom_call" | custom-call | tf_op jit(solution)/shard_map/layer/pallas_call | solution.py:434
  120.8 2.7 %out.1 = (bf16[1,128,4096]{2,1,0:T(8,128)(2,1)}, bf16[1,128,4096]{2,1,0:T(8,128)(2,1)}, bf16[1,128,4096]{2,1,0:T(8,128)(2,1)}, f32[1,1,1024]{2,1,0:T(1,128)}, f3...) custom-call(bf16[1,128,4096]{2,1,0:T(8,128)(2,1)S(1)} %get-tuple-element.14.refs_0_, ...), custom_call_target="tpu_custom_call" | custom-call | tf_op jit(solution)/shard_map/out/pallas_call | solution.py:446

commit v3 on v2

--- a/solution.py
+++ b/solution.py
@@ -11,6 +11,7 @@
 EPS = 1e-06
 VLIM = 56 * 1024 * 1024
 NC = 4
+PG = 2
 BF = jnp.bfloat16
 F32 = jnp.float32
 
@@ -32,9 +33,10 @@
 
 
 def kernel(T, H, *refs):
-    (q, k, v, rates, w1, w2, w3, e) = refs[:8]
+    (q, k, v, rates_in, w1, w2, w3, e) = refs[:8]
     (gq, gk, gv, grates, gf1, gf2, gf3) = refs[8:15]
     (kx, vx, qx, ex, wf, wb, wt, rmat) = refs[15:23]
+    rates, rate_sem = refs[-2:]
     (hid, tgt, d1b, d3b, c1, c2, c3, c4) = refs[23:31]
     (dc1b, dc3b, dbb, gacc, gqb, gkb, gvb, rsum) = refs[31:39]
     (send_a, recv_a, send_1, recv_1, send_2, recv_2, full, ush, dsh, sq_send, sq_recv) = refs[39:50]
@@ -98,6 +100,7 @@
                     else:
                         pltpu.make_async_copy(here, there, in_recv.at[n, m]).start()
 
+    pltpu.make_async_copy(rates_in.at[0], rates, rate_sem).start()
     for j, w in enumerate((w1, w2, w3)):
         pltpu.make_async_copy(w.at[0], wf.at[j], w_sem.at[j]).start()
 
@@ -107,10 +110,12 @@
         wb[j] = wf[j].astype(BF)
         wt[j] = wf[j, :, pl.ds(pl.multiple_of(x * 2 * SH, 2 * SH), 2 * SH)].T.reshape(2, SH, PD)
 
+    arrived(rates, rate_sem)
+
     @pl.loop(0, H)
     def _(i):
         p = head_of(i // 2, lax.rem(i, 2))
-        r = rates[0, :, pl.ds(pl.multiple_of(p * TB, TB), TB)]
+        r = rates[:, pl.ds(pl.multiple_of(p * TB, TB), TB)]
         rmat[i] = jnp.broadcast_to(r, (TB, TB)).T
 
     gacc[...] = jnp.zeros_like(gacc)
@@ -152,94 +157,106 @@
         gacc[0] += mm_tn(db1, kk)
         gacc[2] += mm_tn(db3, kk)
 
-    HF = SH // 2
+    QR = SH // PG
+    HF = QR // 2
+
+    def at(u):
+        return u // PG, (u % PG) * QR
 
     def rows(p):
         return pl.ds(p * HF, HF)
 
-    def cores_start(n, j):
+    def cores_start(n, u):
+        j, lo = at(u)
         g = gacc.at[j].reshape(X, 2, SH, PD)
-        send_a[n, j] = g[:, 1 - c].astype(BF)
-        remote(send_a.at[n, j], recv_a.at[n, j], as_sem.at[n, j], ar_sem.at[n, j], partner).start()
-
-    def chip_sum(n, j, piece, p):
+        send_a[n, u] = g[:, 1 - c, pl.ds(lo, QR)].astype(BF)
+        remote(send_a.at[n, u], recv_a.at[n, u], as_sem.at[n], ar_sem.at[n, u], partner).start()
+
+    def chip_sum(n, u, piece, p):
+        j, lo = at(u)
         g = gacc.at[j].reshape(X, 2, SH, PD)
-        return g[piece, c, rows(p)] + recv_a[n, j, piece, rows(p)].astype(F32)
-
-    def halve_start(n, j):
-        arrived(recv_a.at[n, j], ar_sem.at[n, j])
+        return g[piece, c, pl.ds(lo + p * HF, HF)] + recv_a[n, u, piece, rows(p)].astype(F32)
+
+    def halve_start(n, u):
+        arrived(recv_a.at[n, u], ar_sem.at[n, u])
         for p, near in SIDE:
             for m, piece in enumerate((near, opp)):
-                send_1[n, j, p, m] = chip_sum(n, j, piece, p).astype(BF)
+                send_1[n, u, p, m] = chip_sum(n, u, piece, p).astype(BF)
             remote(
-                send_1.at[n, j, p], recv_1.at[n, j, p], s1_sem.at[n, j, p], r1_sem.at[n, j, p], {"tok": near * 2 + c}
+                send_1.at[n, u, p], recv_1.at[n, u, p], s1_sem.at[n], r1_sem.at[n, u, p], {"tok": near * 2 + c}
             ).start()
 
-    def halve_again(n, j):
+    def halve_again(n, u):
         for p, near in ((0, nb), (1, na)):
-            arrived(recv_1.at[n, j, p], r1_sem.at[n, j, p])
-            send_2[n, j, p] = (chip_sum(n, j, near, p) + recv_1[n, j, p, 1].astype(F32)).astype(BF)
+            arrived(recv_1.at[n, u, p], r1_sem.at[n, u, p])
+            send_2[n, u, p] = (chip_sum(n, u, near, p) + recv_1[n, u, p, 1].astype(F32)).astype(BF)
             remote(
-                send_2.at[n, j, p], recv_2.at[n, j, p], s2_sem.at[n, j, p], r2_sem.at[n, j, p], {"tok": near * 2 + c}
+                send_2.at[n, u, p], recv_2.at[n, u, p], s2_sem.at[n], r2_sem.at[n, u, p], {"tok": near * 2 + c}
             ).start()
 
-    def scatter_end(n, j):
+    def scatter_end(n, u):
         parts = []
         for p in range(2):
-            arrived(recv_2.at[n, j, p], r2_sem.at[n, j, p])
-            parts.append(chip_sum(n, j, x, p) + recv_1[n, j, p, 0].astype(F32) + recv_2[n, j, p].astype(F32))
+            arrived(recv_2.at[n, u, p], r2_sem.at[n, u, p])
+            parts.append(chip_sum(n, u, x, p) + recv_1[n, u, p, 0].astype(F32) + recv_2[n, u, p].astype(F32))
         return jnp.concatenate(parts, axis=0)
 
     def send_rows(ref, ss, rs, dev):
         remote(ref, ref, ss, rs, dev).start()
 
-    def gather_start(n, j, val):
-        full[n, j, t] = val.astype(BF)
-        mine = full.at[n, j, t]
+    def gather_start(n, u, val):
+        j, lo = at(u)
+        mine = full.at[n, j, t, pl.ds(lo, QR)]
+        mine[...] = val.astype(BF)
         for p, near in SIDE:
-            send_rows(mine, gs1_sem.at[n, j, p], gr1_sem.at[n, j, p], {"tok": near * 2 + c})
-        send_rows(mine, fs_sem.at[n, j, 0], fr_sem.at[n, j, 0], partner)
-
-    def gather_mid(n, j):
+            send_rows(mine, gs1_sem.at[n], gr1_sem.at[n, u, p], {"tok": near * 2 + c})
+        send_rows(mine, fs_sem.at[n], fr_sem.at[n, j], partner)
+
+    def gather_mid(n, u):
+        j, lo = at(u)
         for p, near in SIDE:
-            got = full.at[n, j, near * 2 + c]
-            arrived(got, gr1_sem.at[n, j, p])
+            got = full.at[n, j, near * 2 + c, pl.ds(lo, QR)]
+            arrived(got, gr1_sem.at[n, u, p])
             q, far = 1 - p, (nb, na)[p]
-            send_rows(got.at[rows(q)], gs2_sem.at[n, j, q], gr2_sem.at[n, j, q], {"tok": far * 2 + c})
-            send_rows(got, fs_sem.at[n, j, 1 + p], fr_sem.at[n, j, 1 + p], partner)
-
-    def gather_far(n, j):
+            half = full.at[n, j, near * 2 + c, pl.ds(lo + q * HF, HF)]
+            send_rows(half, gs2_sem.at[n], gr2_sem.at[n, u, q], {"tok": far * 2 + c})
+            send_rows(got, fs_sem.at[n], fr_sem.at[n, j], partner)
+
+    def gather_far(n, u):
+        j, lo = at(u)
         for p in range(2):
-            got = full.at[n, j, opp * 2 + c, rows(p)]
-            arrived(got, gr2_sem.at[n, j, p])
-            send_rows(got, fs_sem.at[n, j, 3 + p], fr_sem.at[n, j, 3 + p], partner)
+            arrived(full.at[n, j, opp * 2 + c, pl.ds(lo + p * HF, HF)], gr2_sem.at[n, u, p])
+        send_rows(full.at[n, j, opp * 2 + c, pl.ds(lo, QR)], fs_sem.at[n], fr_sem.at[n, j], partner)
 
     def gather_end(n, j):
-        for m, piece in enumerate((x, na, nb)):
-            arrived(full.at[n, j, piece * 2 + 1 - c], fr_sem.at[n, j, m])
-        for p in range(2):
-            arrived(full.at[n, j, opp * 2 + 1 - c, rows(p)], fr_sem.at[n, j, 3 + p])
+        arrived(full.at[n, j, pl.ds(0, X)], fr_sem.at[n, j])
 
     JS = (1, 0, 2)
+    US = [j * PG + b for j in JS for b in range(PG)]
 
     def each(step, n):
+        for u in US:
+            step(n, u)
+
+    def end(n):
         for j in JS:
-            step(n, j)
+            gather_end(n, j)
 
     each(cores_start, 0)
     each(halve_start, 0)
     each(halve_again, 0)
-    for j in JS:
-        w = wt[j, c]
-        u = w - scatter_end(0, j)
+    for z in US:
+        j, lo = at(z)
+        w = wt[j, c, pl.ds(lo, QR)]
+        u = w - scatter_end(0, z)
         rn = jnp.sqrt(jnp.sum(w * w, axis=1, keepdims=True) + EPS)
         un = jnp.sqrt(jnp.sum(u * u, axis=1, keepdims=True) + EPS)
-        ush[j] = u
-        gather_start(0, j, u * (rn / un))
+        ush[j, pl.ds(lo, QR)] = u
+        gather_start(0, z, u * (rn / un))
     gacc[...] = jnp.zeros_like(gacc)
     each(gather_mid, 0)
     each(gather_far, 0)
-    each(gather_end, 0)
+    end(0)
 
     def whole(n, j):
         return full[n, j].reshape(PD, PD)
@@ -286,20 +303,21 @@
         send_back(0, gqb, gq, m)
 
     each(halve_again, 1)
-    for j in JS:
-        w = wt[j, c]
-        u = ush[j]
-        dnew = scatter_end(1, j)
+    for z in US:
+        j, lo = at(z)
+        w = wt[j, c, pl.ds(lo, QR)]
+        u = ush[j, pl.ds(lo, QR)]
+        dnew = scatter_end(1, z)
         rn = jnp.sqrt(jnp.sum(w * w, axis=1, keepdims=True) + EPS)
         un = jnp.sqrt(jnp.sum(u * u, axis=1, keepdims=True) + EPS)
         moment = jnp.sum(dnew * u, axis=1, keepdims=True)
         factor = rn / un
         du = factor * dnew - u * (factor * moment / (un * un))
-        dsh[j] = w * (moment / (un * rn)) + du
-        gather_start(1, j, -du)
+        dsh[j, pl.ds(lo, QR)] = w * (moment / (un * rn)) + du
+        gather_start(1, z, -du)
     each(gather_mid, 1)
     each(gather_far, 1)
-    each(gather_end, 1)
+    end(1)
 
     @pl.loop(0, NC)
     def _(m):
@@ -326,7 +344,8 @@
 
     for j, (left, right) in ((1, (tgt, dbb)), (0, (dc1b, kx)), (2, (dc3b, kx))):
         gacc[j] = mm_tn(left[...].reshape(H * TB, PD), right[...].reshape(H * TB, PD))
-        cores_start(2, j)
+        for b in range(PG):
+            cores_start(2, j * PG + b)
     each(halve_start, 2)
 
     @pl.loop(0, NC)
@@ -336,13 +355,16 @@
         )
         put(gkb, m, g.astype(BF))
         send_back(1, gkb, gk, m, (0,))
+        pl.when(m < 1)(lambda: send_back(1, gkb, gk, m, (1,)))
 
     each(halve_again, 2)
-    for j in JS:
-        sq_send[j] = (scatter_end(2, j) + dsh[j]).astype(BF)
-        remote(sq_send.at[j], sq_recv.at[j], qs_sem.at[j], qr_sem.at[j], other_seq).start()
-
-    @pl.loop(0, NC)
+    for u in US:
+        j, lo = at(u)
+        mine, theirs = sq_send.at[j, pl.ds(lo, QR)], sq_recv.at[j, pl.ds(lo, QR)]
+        mine[...] = (scatter_end(2, u) + dsh[j, pl.ds(lo, QR)]).astype(BF)
+        remote(mine, theirs, qs_sem, qr_sem.at[u], other_seq).start()
+
+    @pl.loop(1, NC)
     def _(m):
         send_back(1, gkb, gk, m, (1,))
 
@@ -351,9 +373,11 @@
         p = head_of(i // 2, lax.rem(i, 2))
         grates[0, :, pl.ds(pl.multiple_of(p * TB, TB), TB)] = -jnp.sum(rsum[i].T, axis=0, keepdims=True)
 
-    for j in JS:
-        arrived(sq_recv.at[j], qr_sem.at[j])
-        gather_start(2, j, sq_send[j].astype(F32) + sq_recv[j].astype(F32))
+    for u in US:
+        j, lo = at(u)
+        mine, theirs = sq_send.at[j, pl.ds(lo, QR)], sq_recv.at[j, pl.ds(lo, QR)]
+        arrived(theirs, qr_sem.at[u])
+        gather_start(2, u, mine[...].astype(F32) + theirs[...].astype(F32))
     each(gather_mid, 2)
     each(gather_far, 2)
     outs = (gf1, gf2, gf3)
@@ -373,18 +397,13 @@
             arrived(src.at[pl.ds(1, H - 1), part(m)], in_send.at[n, m])
 
     for n in range(3):
-        for j in range(3):
-            arrived(send_a.at[n, j], as_sem.at[n, j])
-            for p in range(2):
-                arrived(send_1.at[n, j, p], s1_sem.at[n, j, p])
-                arrived(send_2.at[n, j, p], s2_sem.at[n, j, p])
-                arrived(full.at[n, j, 0], gs1_sem.at[n, j, p])
-                arrived(full.at[n, j, 0, rows(p)], gs2_sem.at[n, j, p])
-                arrived(full.at[n, j, 0, rows(p)], fs_sem.at[n, j, 3 + p])
-            for m in range(3):
-                arrived(full.at[n, j, 0], fs_sem.at[n, j, m])
-    for j in range(3):
-        arrived(sq_send.at[j], qs_sem.at[j])
+        arrived(send_a.at[n], as_sem.at[n])
+        arrived(send_1.at[n], s1_sem.at[n])
+        arrived(send_2.at[n], s2_sem.at[n])
+        arrived(full.at[n, :, pl.ds(0, 2)], gs1_sem.at[n])
+        arrived(full.at[n, :, 0], gs2_sem.at[n])
+        arrived(full.at[n, :, pl.ds(0, X)], fs_sem.at[n])
+    arrived(sq_send, qs_sem)
 
 
 def put_out(*refs):
@@ -418,15 +437,15 @@
             vm(3, pd, pd, dtype=F32), vm(3, pd, pd), vm(3, 2, sh, pd, dtype=F32), vm(H, tb, tb, dtype=F32),
             tok(), tok(), tok(), tok(), tok(F32), tok(F32), tok(F32), tok(F32),
             tok(), tok(), tok(), vm(3, pd, pd, dtype=F32), tok(), tok(), tok(), vm(H, tb, tb, dtype=F32),
-            vm(3, 3, X, sh, pd), vm(3, 3, X, sh, pd),
-            vm(3, 3, 2, 2, sh // 2, pd), vm(3, 3, 2, 2, sh // 2, pd),
-            vm(3, 3, 2, sh // 2, pd), vm(3, 3, 2, sh // 2, pd),
+            vm(3, 3 * PG, X, sh // PG, pd), vm(3, 3 * PG, X, sh // PG, pd),
+            vm(3, 3 * PG, 2, 2, sh // PG // 2, pd), vm(3, 3 * PG, 2, 2, sh // PG // 2, pd),
+            vm(3, 3 * PG, 2, sh // PG // 2, pd), vm(3, 3 * PG, 2, sh // PG // 2, pd),
             vm(3, 3, T, sh, pd), vm(3, sh, pd, dtype=F32), vm(3, sh, pd, dtype=F32),
             vm(3, sh, pd), vm(3, sh, pd),
-            dma((4, NC)), dma((4, NC)), dma((3,)), dma((3, 3)), dma((3, 3)),
-            dma((3, 3, 2)), dma((3, 3, 2)), dma((3, 3, 2)), dma((3, 3, 2)),
-            dma((3, 3, 2)), dma((3, 3, 2)), dma((3, 3, 2)), dma((3, 3, 2)),
-            dma((3, 3, 5)), dma((3, 3, 5)), dma((3,)), dma((3,)), dma((3, NC)), dma((3, NC)),
+            dma((4, NC)), dma((4, NC)), dma((3,)), dma((3,)), dma((3, 3 * PG)),
+            dma((3,)), dma((3, 3 * PG, 2)), dma((3,)), dma((3, 3 * PG, 2)),
+            dma((3,)), dma((3, 3 * PG, 2)), dma((3,)), dma((3, 3 * PG, 2)),
+            dma((3,)), dma((3, 3)), dma(()), dma((3 * PG,)), dma((3, NC)), dma((3, NC)), vm(1, n, dtype=F32), dma(()),
         ]
         anyspace = pl.BlockSpec(memory_space=pl.ANY)
         vmem = pl.BlockSpec(memory_space=pltpu.VMEM)
@@ -434,7 +453,7 @@
         held = pl.pallas_call(
             functools.partial(kernel, T, H),
             out_shape=tuple(pltpu.VMEM(a, b) for a, b in kinds),
-            in_specs=[anyspace, anyspace, anyspace, vmem] + [anyspace] * 4,
+            in_specs=[anyspace] * 8,
             out_specs=(vmem,) * 7,
             scratch_shapes=scratch,
             compiler_params=pltpu.CompilerParams(

time: 124 us -> 120 us (0.968)
  Pallas kernels: 123 us -> 119 us
    pallas_call x1, Pallas kernels: 120 us -> 116 us  [body(): pl.pallas_call(functools.partial(kernel, T, H), out_shape=tuple((pltpu.VM...]
where the time goes in v3:
time: 120 us
  Pallas kernels  119 us (99%)
    pallas_call x1, Pallas kernels, body(): pl.pallas_call(functools.partial(kernel, T, H), out_shape=tuple((pltpu.VM...  116 us
    pallas_call x1, Pallas kernels, body(): pl.pallas_call(put_out, out_shape=tuple((jax.ShapeDtypeStruct(a, b) for a...  2.74 us

profile of v3, /device:TPU:1, one launch (start us, length us, event | category | flops | bytes accessed | tf_op | source)
XLA Modules:
  0.0 119.8 jit_solution(4681175174638190367)
XLA Ops:
  0.6 116.4 %layer.1 = (bf16[1,128,4096]{2,1,0:T(8,128)(2,1)S(1)}, bf16[1,128,4096]{2,1,0:T(8,128)(2,1)S(1)}, bf16[1,128,4096]{2,1,0:T(8,128)(2,1)S(1)}, f32[1,1,1024]{2,1,0...) custom-call(bf16[1,128,4096]{2,1,0:T(8,128)(2,1)} %refs_0_.1, ...), custom_call_target="tpu_custom_call" | custom-call | tf_op jit(solution)/shard_map/layer/pallas_call | solution.py:453
  117.0 2.7 %out.1 = (bf16[1,128,4096]{2,1,0:T(8,128)(2,1)}, bf16[1,128,4096]{2,1,0:T(8,128)(2,1)}, bf16[1,128,4096]{2,1,0:T(8,128)(2,1)}, f32[1,1,1024]{2,1,0:T(1,128)}, f3...) custom-call(bf16[1,128,4096]{2,1,0:T(8,128)(2,1)S(1)} %get-tuple-element.14.refs_0_, ...), custom_call_target="tpu_custom_call" | custom-call | tf_op jit(solution)/shard_map/out/pallas_call | solution.py:465

commit v4 on v3

--- a/solution.py
+++ b/solution.py
@@ -286,7 +286,7 @@
     each(halve_start, 1)
 
     def send_back(n, src, dst, m, which=(0, 1)):
-        for i in range(H):
+        for i in (*range(1, H, 2), *range(2, H, 2), 0):
             dy, dz = i // 2, i % 2
             if dz in which:
                 here = src.at[i, part(m)]

time: 120 us -> 120 us (level)
  no operation moved by 1% of the time
where the time goes in v4:
time: 120 us
  Pallas kernels  119 us (99%)
    pallas_call x1, Pallas kernels, body(): pl.pallas_call(functools.partial(kernel, T, H), out_shape=tuple((pltpu.VM...  116 us
    pallas_call x1, Pallas kernels, body(): pl.pallas_call(put_out, out_shape=tuple((jax.ShapeDtypeStruct(a, b) for a...  2.74 us

profile of v4, /device:TPU:1, one launch (start us, length us, event | category | flops | bytes accessed | tf_op | source)
XLA Modules:
  0.0 119.5 jit_solution(16408436763916777534)
XLA Ops:
  0.6 116.1 %layer.1 = (bf16[1,128,4096]{2,1,0:T(8,128)(2,1)S(1)}, bf16[1,128,4096]{2,1,0:T(8,128)(2,1)S(1)}, bf16[1,128,4096]{2,1,0:T(8,128)(2,1)S(1)}, f32[1,1,1024]{2,1,0...) custom-call(bf16[1,128,4096]{2,1,0:T(8,128)(2,1)} %refs_0_.1, ...), custom_call_target="tpu_custom_call" | custom-call | tf_op jit(solution)/shard_map/layer/pallas_call | solution.py:453
  116.8 2.7 %out.1 = (bf16[1,128,4096]{2,1,0:T(8,128)(2,1)}, bf16[1,128,4096]{2,1,0:T(8,128)(2,1)}, bf16[1,128,4096]{2,1,0:T(8,128)(2,1)}, f32[1,1,1024]{2,1,0:T(1,128)}, f3...) custom-call(bf16[1,128,4096]{2,1,0:T(8,128)(2,1)S(1)} %get-tuple-element.14.refs_0_, ...), custom_call_target="tpu_custom_call" | custom-call | tf_op jit(solution)/shard_map/out/pallas_call | solution.py:465
